TPU v7x, 128 devices: a whole 4x4x4 slice. The times are simulated.
128 devices in a mesh: ep: 4 (over x), tm: 32 (over y, z, core).
Axes of the slice: x: 4, y: 4, z: 4, core: 2. Of those that a mesh axis runs over, the one named last changes fastest.
Arguments:
- predictions: float32 [128, 1048576], P('ep', 'tm'), may hold values from -6 to 6
- leaf_index: int32 [128, 1048576], P('ep', 'tm'), may hold values from 0 to 63
- events: int32 [128, 1048576], P('ep', 'tm'), may hold values 0 or 1
- tie_start: int32 [1048576], P('tm'), may hold values from 0 to 1, as said below
Outputs:
- new_pred: float32 [128, 1048576], P('ep', 'tm')
- leaf_weights: float32 [128, 64], P('ep')
- grad_hess: bfloat16 [2, 128, 32, 32768], P(None, None, 'tm', 'ep')
Inputs may be any that keep to these rules, and one draw needn't show every extreme that they name: `tie_start`: every row whose index is a multiple of 128 begins a tie group.
All inputs are finite; a program needn't handle non-finite values. No bound on the sum of `events` on one device may be relied on, other than what follows from the above.
Results may differ from a plain program's by a relative error of at most 0.0023.
Values may be sent and summed in bfloat16 or wider, within the bound.
A program may use at most 128 MiB of HBM per device.

v0:
```python
import math
import jax
import jax.numpy as jnp
from jax import lax
from jax.sharding import PartitionSpec as P

LEAVES = 64


def prefix(part, axis, combine, identity, reverse):
    count = lax.axis_size(axis)
    place = lax.axis_index(axis)
    ahead = count - 1 - place if reverse else place
    gathered = jax.tree.map(lambda a: lax.all_gather(a, axis), part)
    state = jax.tree.map(lambda a, e: jnp.zeros_like(a) + jnp.asarray(e, a.dtype), part, identity)

    def one(turn, state):
        source = count - 1 - turn if reverse else turn
        return combine(
            state, jax.tree.map(lambda a: lax.dynamic_index_in_dim(a, source, 0, False), gathered)
        )

    return lax.fori_loop(0, ahead, one, state)


def tile_matrices(tie_start):
    length = tie_start.shape[0]
    blocks = length // 128
    starts = tie_start.reshape(blocks, 128)
    labels = jnp.arange(128, dtype=jnp.int32)
    first_local = lax.cummax(jnp.where(starts == 1, labels[None, :], 0), axis=1)
    next_start = jnp.concatenate([starts[:, 1:], jnp.ones((blocks, 1), jnp.int32)], axis=1)
    last_local = lax.cummin(jnp.where(next_start == 1, labels[None, :], 127), axis=1, reverse=True)
    backward = (labels[None, :, None] >= first_local[:, None, :]).astype(jnp.float32)
    forward = (labels[None, :, None] <= last_local[:, None, :]).astype(jnp.float32)
    return (backward, forward)


def block_cumsum(values, matrices, from_end):
    groups = values.shape[0]
    length = values.shape[1]
    blocks = length // 128
    shaped = values.reshape(groups, blocks, 128)
    within = jnp.einsum("ebj,bji->ebi", shaped, matrices, precision=lax.Precision.HIGHEST)
    totals = jnp.sum(shaped, axis=2)
    if from_end:
        offsets = jnp.cumsum(totals[:, ::-1], axis=1)[:, ::-1] - totals
    else:
        offsets = jnp.cumsum(totals, axis=1) - totals
    return (within + offsets[:, :, None]).reshape(groups, length)


def add_values(earlier, later):
    return jax.tree.map(lambda left, right: left + right, earlier, later)


def leaf_partials(leaf_index, gradient, hessian, leaves):
    length = leaf_index.shape[1]
    width = math.gcd(length, 2048)
    labels = jnp.arange(leaves, dtype=jnp.int32)

    def one_block(step, totals):
        start = step * width
        part_leaf = lax.dynamic_slice_in_dim(leaf_index, start, width, 1)
        part_grad = lax.dynamic_slice_in_dim(gradient, start, width, 1)
        part_hess = lax.dynamic_slice_in_dim(hessian, start, width, 1)
        hits = part_leaf[:, None, :] == labels[None, :, None]
        gsum = jnp.sum(jnp.where(hits, part_grad[:, None, :], 0.0), axis=2)
        hsum = jnp.sum(jnp.where(hits, part_hess[:, None, :], 0.0), axis=2)
        return totals + jnp.stack([gsum, hsum], axis=1)

    empty = jnp.zeros((leaf_index.shape[0], 2, leaves), jnp.float32)
    return lax.fori_loop(0, length // width, one_block, empty)


def leaf_lookup(leaf_index, table):
    length = leaf_index.shape[1]
    width = math.gcd(length, 2048)
    labels = jnp.arange(table.shape[1], dtype=jnp.int32)

    def one_block(step, result):
        start = step * width
        part_leaf = lax.dynamic_slice_in_dim(leaf_index, start, width, 1)
        hits = part_leaf[:, None, :] == labels[None, :, None]
        picked = jnp.sum(jnp.where(hits, table[:, :, None], 0.0), axis=1)
        return lax.dynamic_update_slice_in_dim(result, picked, start, 1)

    empty = jnp.zeros(leaf_index.shape, jnp.float32)
    return lax.fori_loop(0, length // width, one_block, empty)


def on_device(predictions, leaf_index, events, tie_start):
    groups = predictions.shape[0]
    length = predictions.shape[1]
    backward, forward = tile_matrices(tie_start)
    weight = jnp.exp(predictions)
    local_risk = block_cumsum(weight, backward, True)
    block_total = local_risk[:, 0]
    zero_column = jnp.zeros((groups,), jnp.float32)
    later_total = prefix(block_total, "tm", add_values, zero_column, True)
    risk = local_risk + later_total[:, None]
    observed = events.astype(jnp.float32)
    inv_one = observed / risk
    inv_two = inv_one / risk
    local_one = block_cumsum(inv_one, forward, False)
    local_two = block_cumsum(inv_two, forward, False)
    totals_pair = (local_one[:, -1], local_two[:, -1])
    earlier_one, earlier_two = prefix(
        totals_pair, "tm", add_values, (zero_column, zero_column), False
    )
    accum_one = local_one + earlier_one[:, None]
    accum_two = local_two + earlier_two[:, None]
    gradient = weight * accum_one - observed
    hessian = weight * accum_one - weight * weight * accum_two
    stacked = jnp.stack([gradient, hessian]).astype(jnp.bfloat16).reshape(2, groups, 1, length)
    grad_hess = lax.all_to_all(stacked, "ep", split_axis=3, concat_axis=1, tiled=True)
    partial_value = leaf_partials(leaf_index, gradient, hessian, LEAVES)
    totals = lax.psum(partial_value, "tm")
    leaf_weights = -totals[:, 0] / (totals[:, 1] + 1.0)
    new_pred = predictions + leaf_lookup(leaf_index, leaf_weights)
    return (new_pred, leaf_weights, grad_hess)


def solution(mesh):
    placed = (P("ep", "tm"), P("ep", "tm"), P("ep", "tm"), P("tm"))
    return jax.shard_map(
        on_device,
        mesh=mesh,
        in_specs=placed,
        out_specs=(P("ep", "tm"), P("ep", None), P(None, None, "tm", "ep")),
        check_vma=False,
    )
```

profile of v0, /device:TPU:2, one launch (start us, length us, event | category | flops | bytes accessed | tf_op | source)
XLA Modules:
  0.0 666.5 jit_solution(1025747727024494581)
XLA Ops:
  0.6 6.2 exponential_bitcast_fusion.1
  12.6 10.0 %fusion.22 = f32[256,4,8,128]{3,2,1,0:T(8,128)S(1)} fusion(f32[4,256,8,128]{3,2,1,0:T(8,128)} %get-tuple-element.397, s32[256,128]{1,0:T(8,128)S(1)} %copy.130, f32[32,256]{0,1:T(8,128)S(1)} %copy.134), kind=kOutput, calls=%fused_computation.44 | convolution fusion | flops 1615855616 | bytes 8552448 | tf_op jit(solution)/shard_map/ebj,bji->ebi/dot_general | solution.py:44
  26.2 68.6 %all-reduce.1 = f32[1024]{0:T(1024)S(1)} all-reduce(f32[1024]{0:T(1024)S(1)} %dynamic-update-slice), channel_id=2, replica_groups=mesh['ep'=4,'tm'=32] {'tm'}, use_global_device_ids=true, to_apply=%add.1 | all-reduce | flops 1024 | bytes 8192
  101.0 9.3 %fusion.34 = (f32[4,8,256,128]{3,1,2,0:T(8,128)}, f32[4,256,8,128]{3,2,1,0:T(8,128)}, f32[4,256,8,128]{3,2,1,0:T(8,128)}, f32[4,8,256,128]{3,1,2,0:T(8,128)S(1)}) fusion(f32[32]{0:T(128)S(1)} %get-tuple-element.296, f32[256,4,8,128]{3,2,1,0:T(8,128)} %copy-done.1, s32[32,32768]{1,0:T(8,128)} %param.14), kind=kLoop, calls=%fused_computation.79 | loop fusion | flops 5242880 | bytes 25165952
  113.4 10.0 %fusion.21 = f32[256,4,8,128]{3,2,1,0:T(8,128)S(1)} fusion(f32[4,256,8,128]{3,2,1,0:T(8,128)} %get-tuple-element.394, s32[256,128]{1,0:T(8,128)S(1)} %copy.128, f32[32,256]{0,1:T(8,128)S(1)} %copy.139), kind=kOutput, calls=%fused_computation.42 | convolution fusion | flops 1615855616 | bytes 8552448 | tf_op jit(solution)/shard_map/ebj,bji->ebi/dot_general | solution.py:44
  130.0 10.0 %fusion.20 = f32[256,4,8,128]{3,2,1,0:T(8,128)S(1)} fusion(f32[4,256,8,128]{3,2,1,0:T(8,128)} %get-tuple-element.393, s32[256,128]{1,0:T(8,128)S(1)} %copy.128, f32[32,256]{0,1:T(8,128)S(1)} %copy.144), kind=kOutput, calls=%fused_computation.40 | convolution fusion | flops 1615855616 | bytes 8552448 | tf_op jit(solution)/shard_map/ebj,bji->ebi/dot_general | solution.py:44
  142.7 64.1 %all-reduce.4 = (f32[1024]{0:T(1024)S(1)}, f32[1024]{0:T(1024)S(1)}) all-reduce(f32[1024]{0:T(1024)S(1)} %dynamic-update-slice.1, f32[1024]{0:T(1024)S(1)} %dynamic-update-slice.2), channel_id=3, replica_groups=mesh['ep'=4,'tm'=32] {'tm'}, use_global_device_ids=true, to_apply=%add.2 | all-reduce | flops 2048 | bytes 16384
  206.9 10.2 %convert_bitcast_fusion = (bf16[1,32,1,32768]{3,1,2,0:T(8,128)(2,1)S(1)}, f32[32,32768]{1,0:T(8,128)}, bf16[1,32,1,32768]{3,1,2,0:T(8,128)(2,1)S(1)}, f32[32,32768]{1,0:T(8,128)}) fusion(f32[32]{0:T(128)S(1)} %get-tuple-element.298, f32[256,4,8,128]{3,2,1,0:T(8,128)} %copy-done.2, f32[32]{0:T(128)S(1)} %get-tuple-element.297, f32[256,4,8,128]{3,2,1,0:T(8,128)} %copy-done, ...), kind=kLoop, calls=%fused_computation.52 | loop fusion | flops 10485760 | bytes 29360384 | tf_op jit(solution)/shard_map/stack | solution.py:115
  219.5 33.0 %copy.146 = bf16[2,32,1,32768]{1,0,2,3:T(2,128)(2,1)} copy(bf16[2,32,1,32768]{3,1,2,0:T(8,128)(2,1)} %pad_maximum_fusion) | data formatting | bytes 8388608 | tf_op jit(solution)/shard_map/stack | solution.py:115
  252.5 19.2 %reshape.184 = bf16[4,2,262144]{2,1,0:T(2,128)(2,1)} reshape(bf16[32768,1,2,32]{3,2,1,0:T(2,128)(2,1)} %bitcast.143) | data formatting | bytes 8388608
  271.7 5.3 all-to-all-start
  277.1 117.7 %while.55 = (s32[]{:T(128)}, f32[32,2,64]{2,0,1:T(8,128)S(1)}, s32[32,32768]{1,0:T(8,128)}, f32[32,32768]{1,0:T(8,128)}, f32[32,32768]{1,0:T(8,128)}, /*index=5*/s32[]{:T(128)}, s32[]{:T(128)}, s32[]{:T(128)}, s32[]{:T(128)}) while((s32[]{:T(128)}, f32[32,2,64]{2,0,1:T(8,128)S(1)}, s32[32,32768]{1,0:T(8,128)}, ...), condition=%wide.region_18.19_spmd.clone, body=%wide.region_15.18_spmd.clone.sunk | while | flops 20979716 | bytes 2424997 | solution.py:73
  279.1 5.3 fusion.39
  286.5 5.3 fusion.39
  323.2 5.3 fusion.39
  330.6 5.3 fusion.39
  337.9 5.3 fusion.39
  374.7 5.3 fusion.39
  394.7 124.3 %psum.7 = f32[32,2,64]{2,0,1:T(8,128)S(1)} all-reduce(f32[32,2,64]{2,0,1:T(8,128)S(1)} %get-tuple-element.299), channel_id=1, replica_groups=mesh['ep'=4,'tm'=32] {'tm'}, use_global_device_ids=true, to_apply=%region_19.20 | all-reduce | flops 4096 | bytes 32768 | tf_op jit(solution)/shard_map/psum | solution.py:118
  521.3 80.5 %while.54 = (s32[]{:T(128)}, f32[32,32768]{1,0:T(8,128)}, s32[32,32768]{1,0:T(8,128)}, f32[32,64]{1,0:T(8,128)S(1)}, s32[]{:T(128)}, /*index=5*/s32[]{:T(128)}, s32[]{:T(128)}, s32[]{:T(128)}) while((s32[]{:T(128)}, f32[32,32768]{1,0:T(8,128)}, s32[32,32768]{1,0:T(8,128)}, f32[32,64]{1,0:T(8,128)S(1)}, s32[]{:T(128)}, ...), condition=%wide.region_22.23_spmd.clone, body=%wide.region_20.22_spmd.clone.sunk | while | flops 12517382 | bytes 1581203 | solution.py:89
  601.8 5.9 add.165
  607.7 12.0 %reshape.185 = bf16[32768,1,2,32]{3,2,1,0:T(2,128)(2,1)} reshape(bf16[4,2,262144]{2,1,0:T(2,128)(2,1)} %all-to-all-done) | data formatting | bytes 8388608
  619.7 40.0 %copy.150 = bf16[2,32,1,4,8192]{4,3,1,0,2:T(4,128)(2,1)} copy(bf16[2,32,1,4,8192]{1,0,4,3,2:T(2,128)(2,1)} %bitcast.144) | data formatting | bytes 8388608 | tf_op jit(solution)/shard_map/all_to_all | solution.py:116
  659.8 6.5 copy.148
  (216 shorter events, 198.2 us)
Async XLA Ops:
  0.6 6.2 copy-start.5
  22.6 2.0 copy-start.1
  22.6 2.1 copy-start.6
  123.4 2.1 copy-start
  123.4 3.7 copy-start.3
  140.0 2.0 copy-start.2
  271.7 336.0 %all-to-all-start = ((bf16[4,2,262144]{2,1,0:T(2,128)(2,1)}), bf16[4,2,262144]{2,1,0:T(2,128)(2,1)}, u32[]{:S(2)}, u32[]{:S(2)}) async-start(bf16[4,2,262144]{2,1,0:T(2,128)(2,1)} %reshape.184), calls=%async_computation | async-start | bytes 8388608 | tf_op jit(solution)/shard_map/all_to_all | solution.py:116
  601.8 5.9 copy-start.4
where the time goes:
time: 677 us; the launch traced here: 666 us
  blocking collectives  257 us (38%)
  local copies, waits for them, and re-layouts  195 us (29%)
  other arithmetic  176 us (26%)
  matrix products  30 us (4%)
    unnamed x2, blocking collectives  133 us
    psum x1, blocking collectives, on_device(): totals = lax.psum(partial_value, 'tm')  124 us
    reduce_sum x16, other arithmetic, one_block(): gsum = jnp.sum(jnp.where(hits, part_grad[:, None, :], 0.0), axis=2)  84.3 us
    reduce_sum x16, other arithmetic, one_block(): picked = jnp.sum(jnp.where(hits, table[:, :, None], 0.0), axis=1)  53.2 us
    unnamed x27, local copies, waits for them, and re-layouts  49.8 us
    all_to_all x2, local copies, waits for them, and re-layouts, on_device(): lax.all_to_all(stacked, 'ep', split_axis=3, concat_axis=1, tiled=True)  46.5 us
    another operation x1, local copies, waits for them, and re-layouts, on_device(): jnp.stack([gradient, hessian]).astype(jnp.bfloat16)  33 us
    dynamic_slice x32, local copies, waits for them, and re-layouts, one_block(): part_leaf = lax.dynamic_slice_in_dim(leaf_index, start, width, 1)  31.1 us
  transfers between devices with their start and end apart: 1, of which 0 were waited for; matrix products, arithmetic and copies ran while one was open for 31% of the time, Pallas kernels for 0%

commit v1 on v0

--- a/solution.py
+++ b/solution.py
@@ -5,6 +5,12 @@
 from jax.sharding import PartitionSpec as P
 
 LEAVES = 64
+
+
+def gather_and_add(x, mesh_axis):
+    parts = lax.all_gather(x, mesh_axis, axis=0, tiled=False)
+    total = parts.sum(axis=0)
+    return total
 
 
 def prefix(part, axis, combine, identity, reverse):
@@ -115,7 +121,7 @@
     stacked = jnp.stack([gradient, hessian]).astype(jnp.bfloat16).reshape(2, groups, 1, length)
     grad_hess = lax.all_to_all(stacked, "ep", split_axis=3, concat_axis=1, tiled=True)
     partial_value = leaf_partials(leaf_index, gradient, hessian, LEAVES)
-    totals = lax.psum(partial_value, "tm")
+    totals = gather_and_add(partial_value, "tm")
     leaf_weights = -totals[:, 0] / (totals[:, 1] + 1.0)
     new_pred = predictions + leaf_lookup(leaf_index, leaf_weights)
     return (new_pred, leaf_weights, grad_hess)

time: 677 us -> 576 us (0.85)
  blocking collectives: 257 us -> 155 us
    psum x1 -> x0, blocking collectives: 124 us -> none  [on_device(): totals = lax.psum(partial_value, 'tm')]
    all_gather x0 -> x1, blocking collectives: none -> 22.1 us  [gather_and_add(): parts = lax.all_gather(x, mesh_axis, axis=0, tiled=False)]
  transfers between devices with their start and end apart: 1 -> 1, of which waited for: 0 -> 0; matrix products, arithmetic and copies ran while one was open for 31% -> 36% of each run, Pallas kernels for 0% -> 0%
where the time goes in v1:
time: 576 us; the launch traced here: 565 us
  local copies, waits for them, and re-layouts  195 us (34%)
  other arithmetic  177 us (31%)
  blocking collectives  155 us (27%)
  matrix products  30 us (5%)
    unnamed x2, blocking collectives  133 us
    reduce_sum x16, other arithmetic, one_block(): gsum = jnp.sum(jnp.where(hits, part_grad[:, None, :], 0.0), axis=2)  84.3 us
    reduce_sum x16, other arithmetic, one_block(): picked = jnp.sum(jnp.where(hits, table[:, :, None], 0.0), axis=1)  53.2 us
    unnamed x27, local copies, waits for them, and re-layouts  49.8 us
    all_to_all x2, local copies, waits for them, and re-layouts, on_device(): lax.all_to_all(stacked, 'ep', split_axis=3, concat_axis=1, tiled=True)  46.5 us
    another operation x1, local copies, waits for them, and re-layouts, on_device(): jnp.stack([gradient, hessian]).astype(jnp.bfloat16)  33 us
    dynamic_slice x32, local copies, waits for them, and re-layouts, one_block(): part_leaf = lax.dynamic_slice_in_dim(leaf_index, start, width, 1)  31.1 us
    dot_general x3, matrix products, block_cumsum(): jnp.einsum('ebj,bji->ebi', shaped, matrices, precision=lax.Precision.HIGH...  30 us
  transfers between devices with their start and end apart: 1, of which 0 were waited for; matrix products, arithmetic and copies ran while one was open for 36% of the time, Pallas kernels for 0%

profile of v1, /device:TPU:2, one launch (start us, length us, event | category | flops | bytes accessed | tf_op | source)
XLA Modules:
  0.0 564.8 jit_solution(10689830349634770257)
XLA Ops:
  0.6 6.2 %exponential_bitcast_fusion.1 = (f32[4,8,256,128]{3,1,2,0:T(8,128)}, f32[4,256,8,128]{3,2,1,0:T(8,128)}) fusion(f32[32,32768]{1,0:T(8,128)} %param.12), kind=kLoop, calls=%fused_computation.51 | loop fusion | bytes 12582912
  12.6 10.0 %fusion.22 = f32[256,4,8,128]{3,2,1,0:T(8,128)S(1)} fusion(f32[4,256,8,128]{3,2,1,0:T(8,128)} %get-tuple-element.397, s32[256,128]{1,0:T(8,128)S(1)} %copy.124, f32[32,256]{0,1:T(8,128)S(1)} %copy.128), kind=kOutput, calls=%fused_computation.44 | convolution fusion | flops 1615855616 | bytes 8552448 | tf_op jit(solution)/shard_map/ebj,bji->ebi/dot_general | solution.py:50
  26.2 68.6 %all-reduce.1 = f32[1024]{0:T(1024)S(1)} all-reduce(f32[1024]{0:T(1024)S(1)} %dynamic-update-slice), channel_id=2, replica_groups=mesh['ep'=4,'tm'=32] {'tm'}, use_global_device_ids=true, to_apply=%add.1 | all-reduce | flops 1024 | bytes 8192
  101.0 9.3 %fusion.33 = (f32[4,8,256,128]{3,1,2,0:T(8,128)}, f32[4,256,8,128]{3,2,1,0:T(8,128)}, f32[4,256,8,128]{3,2,1,0:T(8,128)}, f32[4,8,256,128]{3,1,2,0:T(8,128)S(1)}) fusion(f32[32]{0:T(128)S(1)} %get-tuple-element.296, f32[256,4,8,128]{3,2,1,0:T(8,128)} %copy-done.1, s32[32,32768]{1,0:T(8,128)} %param.14), kind=kLoop, calls=%fused_computation.78 | loop fusion | flops 5242880 | bytes 25165952
  113.4 10.0 %fusion.21 = f32[256,4,8,128]{3,2,1,0:T(8,128)S(1)} fusion(f32[4,256,8,128]{3,2,1,0:T(8,128)} %get-tuple-element.394, s32[256,128]{1,0:T(8,128)S(1)} %copy.122, f32[32,256]{0,1:T(8,128)S(1)} %copy.133), kind=kOutput, calls=%fused_computation.42 | convolution fusion | flops 1615855616 | bytes 8552448 | tf_op jit(solution)/shard_map/ebj,bji->ebi/dot_general | solution.py:50
  130.0 10.0 %fusion.20 = f32[256,4,8,128]{3,2,1,0:T(8,128)S(1)} fusion(f32[4,256,8,128]{3,2,1,0:T(8,128)} %get-tuple-element.393, s32[256,128]{1,0:T(8,128)S(1)} %copy.122, f32[32,256]{0,1:T(8,128)S(1)} %copy.138), kind=kOutput, calls=%fused_computation.40 | convolution fusion | flops 1615855616 | bytes 8552448 | tf_op jit(solution)/shard_map/ebj,bji->ebi/dot_general | solution.py:50
  142.7 64.1 %all-reduce.4 = (f32[1024]{0:T(1024)S(1)}, f32[1024]{0:T(1024)S(1)}) all-reduce(f32[1024]{0:T(1024)S(1)} %dynamic-update-slice.1, f32[1024]{0:T(1024)S(1)} %dynamic-update-slice.2), channel_id=3, replica_groups=mesh['ep'=4,'tm'=32] {'tm'}, use_global_device_ids=true, to_apply=%add.2 | all-reduce | flops 2048 | bytes 16384
  206.9 10.2 %convert_bitcast_fusion = (bf16[1,32,1,32768]{3,1,2,0:T(8,128)(2,1)S(1)}, f32[32,32768]{1,0:T(8,128)}, bf16[1,32,1,32768]{3,1,2,0:T(8,128)(2,1)S(1)}, f32[32,32768]{1,0:T(8,128)}) fusion(f32[32]{0:T(128)S(1)} %get-tuple-element.298, f32[256,4,8,128]{3,2,1,0:T(8,128)} %copy-done.2, f32[32]{0:T(128)S(1)} %get-tuple-element.297, f32[256,4,8,128]{3,2,1,0:T(8,128)} %copy-done, ...), kind=kLoop, calls=%fused_computation.52 | loop fusion | flops 10485760 | bytes 29360384 | tf_op jit(solution)/shard_map/stack | solution.py:121
  219.5 33.0 %copy.141 = bf16[2,32,1,32768]{1,0,2,3:T(2,128)(2,1)} copy(bf16[2,32,1,32768]{3,1,2,0:T(8,128)(2,1)} %pad_maximum_fusion) | data formatting | bytes 8388608 | tf_op jit(solution)/shard_map/stack | solution.py:121
  252.5 19.2 %reshape.185 = bf16[4,2,262144]{2,1,0:T(2,128)(2,1)} reshape(bf16[32768,1,2,32]{3,2,1,0:T(2,128)(2,1)} %bitcast.143) | data formatting | bytes 8388608
  271.7 5.3 all-to-all-start
  277.1 117.7 %while.55 = (s32[]{:T(128)}, f32[32,2,64]{2,0,1:T(8,128)S(1)}, s32[32,32768]{1,0:T(8,128)}, f32[32,32768]{1,0:T(8,128)}, f32[32,32768]{1,0:T(8,128)}, /*index=5*/s32[]{:T(128)}, s32[]{:T(128)}, s32[]{:T(128)}, s32[]{:T(128)}) while((s32[]{:T(128)}, f32[32,2,64]{2,0,1:T(8,128)S(1)}, s32[32,32768]{1,0:T(8,128)}, ...), condition=%wide.region_18.19_spmd.clone, body=%wide.region_15.18_spmd.clone.sunk | while | flops 20979716 | bytes 2424997 | solution.py:79
  279.1 5.3 fusion.38
  286.5 5.3 fusion.38
  323.2 5.3 fusion.38
  330.6 5.3 fusion.38
  337.9 5.3 fusion.38
  374.7 5.3 fusion.38
  394.7 22.1 %all-gather.3 = f32[1024,2,64]{2,1,0:T(2,128)S(1)} all-gather(f32[32,2,64]{2,1,0:T(2,128)S(1)} %copy.140), channel_id=5, replica_groups=mesh['ep'=4,'tm'=32] {'tm'}, dimensions={0}, use_global_device_ids=true | all-gather | bytes 540672 | tf_op jit(solution)/shard_map/all_gather | solution.py:11
  419.6 80.5 %while.54 = (s32[]{:T(128)}, f32[32,32768]{1,0:T(8,128)}, s32[32,32768]{1,0:T(8,128)}, f32[32,64]{1,0:T(8,128)S(1)}, s32[]{:T(128)}, /*index=5*/s32[]{:T(128)}, s32[]{:T(128)}, s32[]{:T(128)}) while((s32[]{:T(128)}, f32[32,32768]{1,0:T(8,128)}, s32[32,32768]{1,0:T(8,128)}, f32[32,64]{1,0:T(8,128)S(1)}, s32[]{:T(128)}, ...), condition=%wide.region_22.23_spmd.clone, body=%wide.region_20.22_spmd.clone.sunk | while | flops 12517382 | bytes 1581203 | solution.py:95
  500.1 5.9 %add.163 = f32[32,32768]{1,0:T(8,128)} add(f32[32,32768]{1,0:T(8,128)} %param.12, f32[32,32768]{1,0:T(8,128)} %get-tuple-element.300) | non-fusion elementwise | flops 1048576 | bytes 12582912 | tf_op jit(solution)/shard_map/add | solution.py:126
  506.0 12.0 %reshape.186 = bf16[32768,1,2,32]{3,2,1,0:T(2,128)(2,1)} reshape(bf16[4,2,262144]{2,1,0:T(2,128)(2,1)} %all-to-all-done) | data formatting | bytes 8388608
  518.0 40.0 %copy.145 = bf16[2,32,1,4,8192]{4,3,1,0,2:T(4,128)(2,1)} copy(bf16[2,32,1,4,8192]{1,0,4,3,2:T(2,128)(2,1)} %bitcast.144) | data formatting | bytes 8388608 | tf_op jit(solution)/shard_map/all_to_all | solution.py:122
  558.1 6.5 %copy.143 = bf16[2,4,32,1,8192]{4,2,1,0,3:T(8,128)(2,1)} copy(bf16[2,4,32,1,8192]{4,1,2,0,3:T(4,128)(2,1)} %bitcast.145) | data formatting | bytes 8388608 | tf_op jit(solution)/shard_map/all_to_all | solution.py:122
  (218 shorter events, 198.7 us)
Async XLA Ops:
  0.6 6.2 %copy-start.5 = (s32[32768]{0:T(1024)S(1)}, s32[32768]{0:T(1024)}, u32[]{:S(2)}) copy-start(s32[32768]{0:T(1024)} %param.15) | copy-start | bytes 393220
  22.6 2.0 copy-start.1
  22.6 2.1 copy-start.6
  123.4 2.1 copy-start
  123.4 3.7 copy-start.3
  140.0 2.0 copy-start.2
  271.7 234.3 %all-to-all-start = ((bf16[4,2,262144]{2,1,0:T(2,128)(2,1)}), bf16[4,2,262144]{2,1,0:T(2,128)(2,1)}, u32[]{:S(2)}, u32[]{:S(2)}) async-start(bf16[4,2,262144]{2,1,0:T(2,128)(2,1)} %reshape.185), calls=%async_computation | async-start | bytes 8388608 | tf_op jit(solution)/shard_map/all_to_all | solution.py:122
  500.1 5.9 %copy-start.4 = (f32[32,64]{1,0:T(8,128)}, f32[32,64]{1,0:T(8,128)S(1)}, u32[]{:S(2)}) copy-start(f32[32,64]{1,0:T(8,128)S(1)} %get-tuple-element.635) | copy-start | bytes 24580
